TPU v7x, 256 devices: a whole 4x4x8 slice. The times are simulated.
256 devices in a mesh: member: 4 (over y), seq: 64 (over z, x, core).
Axes of the slice: x: 4, y: 4, z: 8, core: 2. Of those that a mesh axis runs over, the one named last changes fastest.
Arguments:
- hidden: bfloat16 [4, 24576, 2880], P('member', 'seq'), may hold values from -6 to 6
- segments: int32 [24576], replicated, may hold values from 0 to 127, never falling along the last dimension, each value on 1 to 768 neighbouring positions
- pre_gain: float32 [4, 2880], P('member'), may hold values from 0.5 to 1.5
- w_query: bfloat16 [4, 2880, 2048], P('member', 'seq'), may hold values from -3 to 3
- w_key: bfloat16 [4, 2880, 256], P('member', 'seq'), may hold values from -3 to 3
- w_value: bfloat16 [4, 2880, 256], P('member', 'seq'), may hold values from -0.109375 to 0.109375
- w_output: bfloat16 [4, 2048, 2880], P('member', 'seq'), may hold values from -0.125 to 0.125
- post_gain: float32 [4, 2880], P('member'), may hold values from 0.5 to 1.5
- final_gain: float32 [4, 2880], P('member'), may hold values from 0.5 to 1.5
- w_judge: bfloat16 [4, 2880, 128], P('member'), may hold values from -0.21875 to 0.21875
Outputs:
- residual_out: bfloat16 [4, 24576, 2880], P('member', 'seq')
- logits: float32 [24576, 128], P('seq')
Inputs may be any that keep to these rules, and one draw needn't show every extreme that they name: `segments`: segment numbers never fall from one token to the next; every number is used, each names 1 to 768 consecutive tokens, and one names exactly 768.
All inputs are finite; a program needn't handle non-finite values.
Results may differ from a plain program's by a relative error of at most 0.014.
Values may be sent and summed in bfloat16 or wider, within the bound.
A program may use at most 128 MiB of HBM per device.

v0:
```python
import math

import jax
import jax.numpy as jnp
from jax import lax
from jax.sharding import PartitionSpec as P

QH = 32
KVH = 4
HD = 64
WINDOW = 128


epsilon = 1e-06
softcap = 50.0
rope_base = 10000.0


def from_behind(block, axis, distance):
    devices = range(lax.axis_size(axis))
    route = [(i - distance, i) for i in devices if i - distance in devices]
    return lax.ppermute(block, axis, route)


def rms_norm(inputs, scale_gain):
    values = inputs.astype(jnp.float32)
    return (
        values * lax.rsqrt(jnp.mean(values * values, axis=-1, keepdims=True) + epsilon) * scale_gain
    )


def rotate(inputs, positions):
    head_size = inputs.shape[-1]
    half_dim = head_size // 2
    frequency = jnp.exp(
        jnp.arange(half_dim, dtype=jnp.float32) * (-2.0 * math.log(rope_base) / head_size)
    )
    angles = positions.astype(jnp.float32)[:, None] * frequency[None, :]
    cosine_term = jnp.cos(angles)[:, None, :]
    sine_term = jnp.sin(angles)[:, None, :]
    lower_half = inputs[..., :half_dim]
    upper_half = inputs[..., half_dim:]
    return jnp.concatenate(
        [
            lower_half * cosine_term - upper_half * sine_term,
            upper_half * cosine_term + lower_half * sine_term,
        ],
        axis=-1,
    )


def attend_heads(block_queries, block_keys, block_values, seg_query, seg_key):
    query_count = block_queries.shape[0]
    key_count = block_keys.shape[0]
    head_span = QH // KVH * HD
    distance = (
        jnp.arange(query_count, dtype=jnp.int32)[:, None]
        + (key_count - query_count)
        - jnp.arange(key_count, dtype=jnp.int32)[None, :]
    )
    allowed = (distance >= 0) & (distance < WINDOW) & (seg_query[:, None] == seg_key[None, :])

    def one_head(head_index):
        query_head = lax.dynamic_slice_in_dim(
            block_queries, head_index * head_span, head_span, 1
        ).reshape(query_count, QH // KVH, HD)
        key_head = lax.dynamic_slice_in_dim(block_keys, head_index * HD, HD, 1)
        value_head = lax.dynamic_slice_in_dim(block_values, head_index * HD, HD, 1)
        scores = jnp.einsum("qgd,kd->gqk", query_head, key_head, preferred_element_type=jnp.float32)
        scores = softcap * jnp.tanh(scores / softcap)
        expanded = jnp.where(allowed[None], jnp.exp(scores), 0.0)
        weights = (expanded / jnp.sum(expanded, axis=-1, keepdims=True)).astype(jnp.bfloat16)
        head_out = jnp.einsum(
            "gqk,kd->qgd", weights, value_head, preferred_element_type=jnp.float32
        )
        return head_out.astype(jnp.bfloat16).reshape(query_count, head_span)

    per_head = lax.map(one_head, jnp.arange(KVH, dtype=jnp.int32))
    return per_head.transpose(1, 0, 2).reshape(query_count, KVH * head_span)


def body(
    hidden, segments, pre_gain, w_query, w_key, w_value, w_output, post_gain, final_gain, w_judge
):
    tok_rows = hidden.shape[1]
    dev_index = lax.axis_index("seq")
    row_first = dev_index * tok_rows
    own_rows = hidden[0]
    normed = rms_norm(own_rows, pre_gain[0]).astype(jnp.bfloat16)
    kv_count = normed.shape[0]
    queries = jnp.dot(
        normed,
        lax.all_gather(w_query[0], "seq", axis=0, tiled=True),
        preferred_element_type=jnp.float32,
    )
    key_rows = jnp.dot(
        normed,
        lax.all_gather(w_key[0], "seq", axis=0, tiled=True),
        preferred_element_type=jnp.float32,
    )
    val_rows = jnp.dot(
        normed,
        lax.all_gather(w_value[0], "seq", axis=0, tiled=True),
        preferred_element_type=jnp.float32,
    )
    query_positions = row_first + jnp.arange(tok_rows, dtype=jnp.int32)
    key_positions = row_first - (kv_count - tok_rows) + jnp.arange(kv_count, dtype=jnp.int32)
    queries = (
        (rotate(queries.reshape(tok_rows, QH, HD), query_positions) * (1.0 / math.sqrt(HD)))
        .astype(jnp.bfloat16)
        .reshape(tok_rows, QH * HD)
    )
    key_rows = (
        rotate(key_rows.reshape(kv_count, KVH, HD), key_positions)
        .astype(jnp.bfloat16)
        .reshape(kv_count, KVH * HD)
    )
    val_rows = val_rows.astype(jnp.bfloat16)
    earlier_keys, earlier_values = from_behind(
        (key_rows[tok_rows - WINDOW :], val_rows[tok_rows - WINDOW :]), "seq", 1
    )
    key_rows = jnp.concatenate([earlier_keys, key_rows], axis=0)
    val_rows = jnp.concatenate([earlier_values, val_rows], axis=0)
    seg_own = lax.dynamic_slice_in_dim(segments, row_first, tok_rows, 0)
    seg_prior = lax.dynamic_slice_in_dim(segments, jnp.maximum(row_first - WINDOW, 0), WINDOW, 0)
    seg_prior = jnp.where(dev_index > 0, seg_prior, -1)
    seg_keys = jnp.concatenate([seg_prior, seg_own], axis=0)
    block_rows = min(tok_rows, 512)

    def one_block(block_number):
        return attend_heads(queries, key_rows, val_rows, seg_own, seg_keys)

    attended = lax.map(one_block, jnp.arange(tok_rows // block_rows, dtype=jnp.int32)).reshape(
        tok_rows, QH * HD
    )
    projected = jnp.dot(
        attended,
        lax.all_gather(w_output[0], "seq", axis=0, tiled=True),
        preferred_element_type=jnp.float32,
    )
    updated = (own_rows.astype(jnp.float32) + rms_norm(projected, post_gain[0])).astype(
        jnp.bfloat16
    )
    closing = rms_norm(updated, final_gain[0]).astype(jnp.bfloat16)
    verdict = jnp.dot(closing, w_judge[0], preferred_element_type=jnp.float32)
    summed_verdict = lax.psum(verdict.astype(jnp.bfloat16), "member").astype(jnp.float32)
    return (updated[None], summed_verdict / lax.axis_size("member"))


def solution(mesh):
    return jax.shard_map(
        body,
        mesh=mesh,
        in_specs=(
            P("member", "seq", None),
            P(),
            P("member", None),
            P("member", "seq", None),
            P("member", "seq", None),
            P("member", "seq", None),
            P("member", "seq", None),
            P("member", None),
            P("member", None),
            P("member", None, None),
        ),
        out_specs=(P("member", "seq", None), P("seq", None)),
        check_vma=False,
    )
```

profile of v0, /device:TPU:1, one launch (start us, length us, event | category | flops | bytes accessed | tf_op | source)
XLA Modules:
  0.0 455.6 jit_solution(2094596954263053369)
XLA Ops:
  10.3 2.0 copy.27
  16.8 2.2 fusion.27
  19.2 74.3 %all-gather.9.cloned.1.call-done = bf16[1,2880,256]{2,0,1:T(2,128)(2,1)} async-done(((bf16[1,45,256]{2,0,1:T(2,128)(2,1)}), bf16[1,2880,256]{2,0,1:T(2,128)(2,1)}) %all-gather.9.cloned.1.call-update) | async-done | bytes 1474576 | tf_op jit(solution)/shard_map/all_gather | solution.py:103
  93.5 3.2 fusion.45
  97.5 2.1 collective-permute-start
  99.5 72.1 %all-gather.11.cloned.1.call-done = bf16[1,2880,256]{2,0,1:T(2,128)(2,1)} async-done(((bf16[1,45,256]{2,0,1:T(2,128)(2,1)}), bf16[1,2880,256]{2,0,1:T(2,128)(2,1)}) %all-gather.11.cloned.1.call-update) | async-done | bytes 1474576 | tf_op jit(solution)/shard_map/all_gather | solution.py:98
  171.6 7.3 %copy.34 = bf16[1,2880,256]{1,2,0:T(8,128)(2,1)} copy(bf16[1,2880,256]{2,0,1:T(2,128)(2,1)} %all-gather.11.cloned.1.call-done) | data formatting | bytes 2949120 | tf_op jit(solution)/shard_map/dot_general | solution.py:96
  178.9 2.5 fusion.56
  182.2 2.3 collective-permute-start.1
  188.5 99.7 %all-gather.13.cloned.1.call-done = bf16[1,2880,2048]{2,0,1:T(2,128)(2,1)} async-done(((bf16[1,45,2048]{2,0,1:T(2,128)(2,1)}), bf16[1,2880,2048]{2,0,1:T(2,128)(2,1)}) %all-gather.13.cloned.1.call-update) | async-done | bytes 11796496 | tf_op jit(solution)/shard_map/all_gather | solution.py:93
  288.1 50.9 %copy.35 = bf16[1,2880,2048]{1,2,0:T(8,128)(2,1)} copy(bf16[1,2880,2048]{2,0,1:T(2,128)(2,1)} %all-gather.13.cloned.1.call-done) | data formatting | bytes 23592960 | tf_op jit(solution)/shard_map/dot_general | solution.py:91
  339.0 9.7 %fusion.54 = f32[384,32,64]{0,2,1:T(8,128)S(1)} fusion(bf16[32,64,2880]{2,1,0:T(8,128)(2,1)} %bitcast.102, bf16[1,384,2880]{1,2,0:T(8,128)(2,1)S(1)} %copy-done.1, f32[2880]{0:T(1024)S(1)} %reduce, f32[384]{0:T(512)S(1)} %copy-done.6), kind=kOutput, calls=%fused_computation.58 | convolution fusion | flops 4534272000 | bytes 17167104 | tf_op jit(solution)/shard_map/dot_general | solution.py:91
  350.7 40.1 %while.18 = (s32[]{:T(128)}, bf16[4,384,512]{1,2,0:T(8,128)(2,1)}, s32[4]{0:T(128)S(1)}, bf16[512,256]{0,1:T(8,128)(2,1)}, bf16[512,256]{0,1:T(8,128)(2,1)}, /*i...) while((s32[]{:T(128)}, bf16[4,384,512]{1,2,0:T(8,128)(2,1)}, ...), condition=%wide.region_3.4_spmd.clone, body=%wide.region_1.3_spmd.clone.sunk | while | flops 418182144 | bytes 15693569 | solution.py:78
  353.9 3.0 fusion.71
  357.0 3.0 fusion.72
  364.0 3.0 fusion.71
  367.0 3.0 fusion.72
  374.0 3.0 fusion.71
  377.0 3.0 fusion.72
  384.0 3.0 fusion.71
  387.1 3.0 fusion.72
  390.8 10.0 %multiply_reduce_fusion = (f32[384]{0:T(512)S(1)}, f32[384,2880]{0,1:T(8,128)S(1)}) fusion(bf16[384,2048]{0,1:T(8,128)(2,1)} %bitcast.11, bf16[1,2048,2880]{2,1,0:T(8,128)(2,1)} %all-gather.15.cloned.1.call-done), kind=kOutput, calls=%fused_computation.41 | convolution fusion | flops 4532059648 | bytes 17794560 | tf_op jit(solution)/shard_map/dot_general | solution.py:136
  403.7 2.1 fusion.50
  405.8 41.7 %all-reduce.2.cloned.1.call-done = bf16[384,128]{1,0:T(8,128)(2,1)} async-done(((bf16[384,128]{1,0:T(8,128)(2,1)}), bf16[384,128]{1,0:T(8,128)(2,1)}) %all-reduce.2.cloned.1.call-update) | async-done | bytes 98320 | tf_op jit(solution)/shard_map/psum | solution.py:146
  (71 shorter events, 30.4 us)
Async XLA Ops:
  7.2 396.5 %copy-start = (bf16[1,2880,128]{2,1,0:T(8,128)(2,1)S(1)}, bf16[1,2880,128]{2,1,0:T(8,128)(2,1)}, u32[]{:S(2)}) copy-start(bf16[1,2880,128]{2,1,0:T(8,128)(2,1)} %param.21) | copy-start | bytes 2211844
  7.2 86.3 %copy-start.1 = (bf16[1,384,2880]{1,2,0:T(8,128)(2,1)S(1)}, bf16[1,384,2880]{1,2,0:T(8,128)(2,1)}, u32[]{:S(2)}) copy-start(bf16[1,384,2880]{1,2,0:T(8,128)(2,1)} %param.12) | copy-start | bytes 6635524
  7.2 86.3 %all-gather.9.cloned.1.call-start = ((), (), s32[]{:S(2)}) async-start(), calls=%async_computation.1 | async-start | bytes 2995200 | tf_op jit(solution)/shard_map/all_gather | solution.py:103
  8.8 162.8 %all-gather.11.cloned.1.call-start = ((), (), s32[]{:S(2)}) async-start(), calls=%async_computation.2 | async-start | bytes 2995200 | tf_op jit(solution)/shard_map/all_gather | solution.py:98
  10.3 277.9 %all-gather.13.cloned.1.call-start = ((), (), s32[]{:S(2)}) async-start(), calls=%async_computation.3 | async-start | bytes 23961600 | tf_op jit(solution)/shard_map/all_gather | solution.py:93
  12.3 378.5 %all-gather.15.cloned.1.call-start = ((), (), s32[]{:S(2)}) async-start(), calls=%async_computation.4 | async-start | bytes 12247040 | tf_op jit(solution)/shard_map/all_gather | solution.py:138
  12.9 434.6 %all-reduce.2.cloned.1.call-start = ((), (), s32[]{:S(2)}) async-start(), calls=%async_computation | async-start | bytes 196608 | tf_op jit(solution)/shard_map/psum | solution.py:146
  19.0 160.0 %copy-start.5 = (f32[384]{0:T(512)}, f32[384]{0:T(512)S(1)}, u32[]{:S(2)}) copy-start(f32[384]{0:T(512)S(1)} %add_rsqrt_fusion.2) | copy-start | bytes 4612
  96.8 0.7 copy-start.3
  97.5 87.0 %collective-permute-start = (bf16[128,256]{1,0:T(8,128)(2,1)S(1)}, bf16[128,256]{1,0:T(8,128)(2,1)}, u32[]{:S(2)}, u32[]{:S(2)}) collective-permute-start(bf16[128,256]{1,0:T(8,128)(2,1)S(1)} %slice.28), channel_id=1, source_target_pairs={{0,1},{1,2},{2,3},{3,4},{4,5},{5,6},{6,7},{7,8},{8,9},{9,10},{10,1... | collective-permute-start | bytes 196616 | tf_op jit(solution)/shard_map/ppermute | solution.py:22
  178.9 5.5 %copy-start.4 = (bf16[384,256]{1,0:T(8,128)(2,1)S(1)}, bf16[384,256]{1,0:T(8,128)(2,1)}, u32[]{:S(2)}) copy-start(bf16[384,256]{1,0:T(8,128)(2,1)} %copy-done.3) | copy-start | bytes 589828
  182.2 4.7 %collective-permute-start.1 = (bf16[128,256]{0,1:T(8,128)(2,1)}, bf16[128,256]{0,1:T(8,128)(2,1)}, u32[]{:S(2)}, u32[]{:S(2)}) collective-permute-start(bf16[128,256]{0,1:T(8,128)(2,1)} %bitcast.5), channel_id=1, source_target_pairs={{0,1},{1,2},{2,3},{3,4},{4,5},{5,6},{6,7},{7,8},{8,9},{9,10},{10,1... | collective-permute-start | bytes 196616 | tf_op jit(solution)/shard_map/ppermute | solution.py:22
  188.5 150.6 %copy-start.6 = (f32[384]{0:T(512)S(1)}, f32[384]{0:T(512)}, u32[]{:S(2)}) copy-start(f32[384]{0:T(512)} %copy-done.5) | copy-start | bytes 4612
  402.3 1.4 copy-start.2
Sparse Core Ops, SparseCore 0:
  11.3 82.2 all-gather.8
  96.2 75.3 all-gather.10
  174.4 113.7 all-gather.12
  290.7 85.5 all-gather.14
  405.9 41.5 all-reduce.1
where the time goes:
time: 460 us; the launch traced here: 456 us
  waiting for transfers between devices  289 us (63%)
  local copies, waits for them, and re-layouts  77.1 us (17%)
  matrix products  51.4 us (11%)
  other arithmetic  14.2 us (3%)
  between operations  14 us (3%)
  loops' own time  5.3 us (1%)
    all_gather x1, waiting for transfers between devices, body(): lax.all_gather(w_query[0], 'seq', axis=0, tiled=True)  99.7 us
    all_gather x1, waiting for transfers between devices, body(): lax.all_gather(w_value[0], 'seq', axis=0, tiled=True)  74.3 us
    all_gather x1, waiting for transfers between devices, body(): lax.all_gather(w_key[0], 'seq', axis=0, tiled=True)  72.1 us
    dot_general x1, local copies, waits for them, and re-layouts, body(): jnp.dot(normed, lax.all_gather(w_query[0], 'seq', axis=0, tiled=True), pr...  50.9 us
    psum x1, waiting for transfers between devices, body(): lax.psum(verdict.astype(jnp.bfloat16), 'member').astype(jnp.float32)  41.7 us
    dot_general x4, matrix products, one_head(): jnp.einsum('qgd,kd->gqk', query_head, key_head, preferred_element_type=jn...  12.1 us
    dot_general x4, matrix products, one_head(): jnp.einsum('gqk,kd->qgd', weights, value_head, preferred_element_type=jnp...  11.9 us
    dot_general x1, matrix products, body(): jnp.dot(attended, lax.all_gather(w_output[0], 'seq', axis=0, tiled=True),...  9.97 us
  transfers between devices with their start and end apart: 7, of which 5 were waited for; matrix products, arithmetic and copies ran while one was open for 27% of the time, Pallas kernels for 0%

commit v1 on v0

v1 whole, which is shorter than its diff:
```python
import math

import jax
import jax.numpy as jnp
from jax import lax
from jax.experimental import pallas as pl
from jax.experimental.pallas import tpu as pltpu
from jax.sharding import PartitionSpec as P

QH = 32
KVH = 4
HD = 64
WINDOW = 128
D = 2880
TOK = 384
XN = 4
ZN = 8
MEM = 4
BQ = 48
BO = 32
NQ = KVH * HD * 2 + QH * HD
CQ = 1024
CO = 1152

epsilon = 1e-06
softcap = 50.0
rope_base = 10000.0

f32 = jnp.float32
bf16 = jnp.bfloat16
MESH = pl.DeviceIdType.MESH


def mod(a, n):
    return lax.rem(a + n, n)


def kernel(
    hid,
    seg,
    pre_g,
    wqkv,
    wo,
    post_g,
    fin_g,
    wj,
    res_out,
    logit_out,
    WQ,
    WO,
    HID,
    SEG,
    PRE,
    POST,
    FIN,
    WJ,
    NRM,
    A,
    COS,
    SIN,
    Q,
    KV,
    HALO,
    KD,
    VD,
    ATT,
    PRJ,
    RES,
    VS,
    LOG,
    local_sem,
    qx,
    qz,
    qpz,
    qpx,
    ox,
    oz,
    opz,
    opx,
    d2d_recv,
    send_sem,
    halo_send,
    halo_recv,
    vs_send,
    vs_recv,
    out_sem,
):
    me = lax.axis_index("seq")
    mem = lax.axis_index("member")
    c = lax.rem(me, 2)
    x = lax.rem(me // 2, XN)
    z = me // (2 * XN)
    s = 1 - 2 * c

    def seq_of(zz, xx, cc):
        return (zz * XN + xx) * 2 + cc

    x_f = seq_of(z, mod(x + s, XN), c)
    x_b = seq_of(z, mod(x - s, XN), c)
    z_f = seq_of(mod(z + s, ZN), x, c)
    z_b = seq_of(mod(z - s, ZN), x, c)
    partner = seq_of(z, x, 1 - c)
    after = mod(me + 1, 64)
    before = mod(me - 1, 64)
    far = jnp.where(c == 0, before, after)

    def local(i, src, dst):
        return pltpu.make_async_copy(src, dst, local_sem.at[i])

    def own(buf, rows):
        return buf.at[pl.ds(pl.multiple_of(me * rows, rows), rows), :]

    loads = [
        local(0, wqkv, own(WQ, BQ)),
        local(1, wo, own(WO, BO)),
        local(2, hid, HID),
        local(3, pre_g, PRE),
        local(4, seg, SEG),
        local(5, post_g, POST),
        local(6, fin_g, FIN),
        local(7, wj, WJ),
    ]
    for load in loads:
        load.start()

    barrier = pltpu.get_barrier_semaphore()
    for peer in (x_f, x_b, z_f, z_b, partner, far):
        pl.semaphore_signal(barrier, inc=1, device_id={"seq": peer}, device_id_type=MESH)
    for delta in (1, 2, 3):
        pl.semaphore_signal(
            barrier, inc=1, device_id={"member": mod(mem + delta, MEM)}, device_id_type=MESH
        )
    pl.semaphore_wait(barrier, 9)

    def z_order(i):
        return mod(z + s * ((i + 1) // 2) * (1 - 2 * lax.rem(i, 2)), ZN)

    def x_order(i):
        return mod(x + s * ((i + 1) // 2) * (1 - 2 * lax.rem(i, 2)), XN)

    class Gather:
        def __init__(self, number, buf, rows, cut, rx, rz, pz, px):
            self.number, self.buf, self.rows, self.cut = number, buf, rows, cut
            self.width = buf.shape[1]
            self.rx, self.rz, self.pz, self.px = rx, rz, pz, px

        def block(self, part, zz, xx):
            first = pl.multiple_of(seq_of(zz, xx, c) * self.rows, self.rows)
            columns = pl.ds(0, self.cut) if part == 0 else pl.ds(self.cut, self.width - self.cut)
            return self.buf.at[pl.ds(first, self.rows), columns]

        def copy(self, part, zz, xx, recv, peer):
            ref = self.block(part, zz, xx)
            return pltpu.make_async_remote_copy(
                src_ref=ref,
                dst_ref=ref,
                send_sem=send_sem.at[self.number],
                recv_sem=recv,
                device_id={"seq": peer},
                device_id_type=MESH,
            )

        def send(self, part, zz, xx, recv, peer):
            self.copy(part, zz, xx, recv, peer).start()

        def wait(self, part, zz, xx, recv):
            self.copy(part, zz, xx, recv, partner).wait_recv()

        def share(self, part, zz, xx):
            self.send(part, zz, xx, d2d_recv.at[self.number], partner)

        def begin(self):
            self.send(0, z, x, self.rx.at[0], x_f)
            self.send(0, z, x, self.rx.at[1], x_b)
            self.send(1, z, x, self.pz.at[0], z_f)
            self.send(1, z, x, self.pz.at[1], z_b)
            self.send(1, z, x, self.px.at[0], x_f)
            self.send(1, z, x, self.px.at[16], x_b)
            self.send(0, z, x, self.rz.at[0], z_f)
            self.send(0, z, x, self.rz.at[16], z_b)
            self.share(0, z, x)
            self.share(1, z, x)

        def first(self, a):
            zz = z_order(a + 1)
            self.wait(1, zz, x, self.pz.at[a])

            @pl.when(a < 5)
            def _():
                onward = seq_of(mod(z + s * (1 - 2 * lax.rem(a, 2)), ZN), x, c)
                self.send(1, zz, x, self.pz.at[a + 2], onward)

            self.send(1, zz, x, self.px.at[a + 1], x_f)
            self.send(1, zz, x, self.px.at[a + 17], x_b)
            self.share(1, zz, x)

            @pl.when(a < 3)
            def _():
                xx = x_order(a + 1)
                self.wait(0, z, xx, self.rx.at[a])

                @pl.when(a == 0)
                def _():
                    self.send(0, z, xx, self.rx.at[2], x_f)

                self.send(0, z, xx, self.rz.at[a + 1], z_f)
                self.send(0, z, xx, self.rz.at[a + 17], z_b)
                self.share(0, z, xx)

        def second(self, r):
            zz = z_order(lax.rem(r, 8))
            xx = mod(x - s * (1 + r // 8), XN)
            self.wait(1, zz, xx, self.px.at[r])

            @pl.when(r < 8)
            def _():
                self.send(1, zz, xx, self.px.at[r + 8], x_f)

            self.share(1, zz, xx)
            xj = x_order(lax.rem(r, 4))
            zk = mod(z - s * (1 + r // 4), ZN)
            self.wait(0, zk, xj, self.rz.at[r])

            @pl.when(r < 12)
            def _():
                self.send(0, zk, xj, self.rz.at[r + 4], z_f)

            self.share(0, zk, xj)

            @pl.when(r < 8)
            def _():
                xb = mod(x + s, XN)
                self.wait(1, zz, xb, self.px.at[r + 16])
                self.share(1, zz, xb)

            @pl.when(r < 12)
            def _():
                zb = mod(z + s * (1 + r // 4), ZN)
                self.wait(0, zb, xj, self.rz.at[r + 16])

                @pl.when(r < 8)
                def _():
                    self.send(0, zb, xj, self.rz.at[r + 20], z_b)

                self.share(0, zb, xj)

        def finish(self):
            half = self.buf.at[pl.ds(0, 32 * self.rows), :]
            pltpu.make_async_copy(half, half, d2d_recv.at[self.number]).wait()

        def drain(self):
            sent = self.buf.at[pl.ds(0, 63 * self.rows), :]
            pltpu.make_async_copy(sent, sent, send_sem.at[self.number]).wait()

    gq = Gather(0, WQ, BQ, CQ, qx, qz, qpz, qpx)
    go = Gather(1, WO, BO, CO, ox, oz, opz, opx)

    loads[0].wait()
    gq.begin()

    loads[2].wait()
    loads[3].wait()
    NRM[:, pl.ds(2816, 128)] = jnp.zeros((TOK, 128), bf16)

    @pl.loop(0, 6)
    def _(i):
        rows = pl.ds(pl.multiple_of(i * 64, 64), 64)
        values = HID[rows, :].astype(f32)
        scale = lax.rsqrt(jnp.mean(values * values, axis=-1, keepdims=True) + epsilon)
        NRM[rows, pl.ds(0, D)] = (values * scale * PRE[...]).astype(bf16)

    @pl.loop(0, 8)
    def _(t):
        start = (t * 360) // 128 * 128
        lead = t * 360 - start
        column = lax.broadcasted_iota(jnp.int32, (1, 384), 1)
        group = jnp.zeros((1, 384), jnp.int32)
        for k in range(1, 8):
            group += jnp.where(column >= 48 * k, 1, 0)
        source = jnp.where(column - 48 * group < 45, column - 3 * group + lead, -1)
        pick = jnp.where(lax.broadcasted_iota(jnp.int32, (512, 384), 0) == source, 1.0, 0.0)
        window = NRM[:, pl.ds(pl.multiple_of(start, 128), 512)]
        moved = jnp.dot(window, pick.astype(bf16), preferred_element_type=f32)
        A[:, pl.ds(pl.multiple_of(t * 384, 384), 384)] = moved.astype(bf16)

        @pl.when(t < 7)
        def _():
            gq.first(t)

    lane = lax.broadcasted_iota(jnp.int32, (1, 128), 1)
    low_half = lax.rem(lane, 64) < 32
    first_head = lane < 64
    index = lax.rem(lane, 32).astype(f32)
    frequency = jnp.exp(index * (-2.0 * math.log(rope_base) / HD))
    sign = jnp.where(low_half, -1.0, 1.0)

    @pl.loop(0, 3)
    def _(i):
        rows = pl.ds(pl.multiple_of(i * 128, 128), 128)
        position = me * TOK + i * 128 + lax.broadcasted_iota(jnp.int32, (128, 128), 0)
        angle = position.astype(f32) * frequency
        COS[rows, :] = jnp.cos(angle)
        SIN[rows, :] = jnp.sin(angle) * sign

    @pl.loop(0, 10)
    def _(r):
        gq.second(r)

    loads[1].wait()
    go.begin()

    @pl.loop(10, 16)
    def _(r):
        gq.second(r)

    gq.finish()

    def rest(slot):
        @pl.when(slot < 7)
        def _():
            go.first(slot)

        @pl.when(slot >= 7)
        def _():
            go.second(slot - 7)

    def rotated(half):
        swapped = jnp.where(low_half, pltpu.roll(half, 96, 1), pltpu.roll(half, 32, 1))
        return half * COS[...] + swapped * SIN[...]

    def doubled(pair):
        turned = pltpu.roll(pair, 64, 1)
        return jnp.where(first_head, pair, turned), jnp.where(first_head, turned, pair)

    def project(tile):
        columns = pl.ds(pl.multiple_of(tile * 256, 256), 256)
        return jnp.dot(A[...], WQ[:, columns], preferred_element_type=f32)

    own_rows = pl.ds(WINDOW, TOK)
    keys = project(0)
    for p in range(2):
        pair = rotated(keys[:, 128 * p : 128 * p + 128]).astype(bf16)
        KV[:, pl.ds(128 * p, 128)] = pair
        for q, both in enumerate(doubled(pair.astype(f32))):
            KD[own_rows, pl.ds(128 * (2 * p + q), 128)] = both.astype(bf16)
    rest(0)
    vals = project(1)
    for p in range(2):
        pair = vals[:, 128 * p : 128 * p + 128].astype(bf16)
        KV[:, pl.ds(256 + 128 * p, 128)] = pair
        for q, both in enumerate(doubled(pair.astype(f32))):
            VD[own_rows, pl.ds(128 * (2 * p + q), 128)] = both.astype(bf16)
    rest(1)

    halo = pltpu.make_async_remote_copy(
        src_ref=KV.at[pl.ds(TOK - WINDOW, WINDOW), :],
        dst_ref=HALO,
        send_sem=halo_send,
        recv_sem=halo_recv,
        device_id={"seq": after},
        device_id_type=MESH,
    )

    def query_tile(i):
        tile = project(i + 2)
        for p in range(2):
            half = rotated(tile[:, 128 * p : 128 * p + 128]) * (1.0 / math.sqrt(HD))
            Q[:, pl.ds(pl.multiple_of(i * 256 + 128 * p, 128), 128)] = half.astype(bf16)
        rest(i + 2)

    @pl.loop(0, 1)
    def _(i):
        query_tile(i)

    halo.start()

    @pl.loop(1, 8)
    def _(i):
        query_tile(i)

    halo.wait()
    for p in range(2):
        for source, store in ((0, KD), (256, VD)):
            pair = HALO[:, pl.ds(source + 128 * p, 128)].astype(f32)
            for q, both in enumerate(doubled(pair)):
                store[pl.ds(0, WINDOW), pl.ds(128 * (2 * p + q), 128)] = both.astype(bf16)

    loads[4].wait()
    ones = jnp.ones((2 * WINDOW, 128), bf16)
    keep_a = jnp.where(first_head, 1.0, 0.0).astype(bf16)
    keep_b = jnp.where(first_head, 0.0, 1.0).astype(bf16)
    q_index = lax.broadcasted_iota(jnp.int32, (WINDOW, WINDOW), 0)
    k_index = lax.broadcasted_iota(jnp.int32, (WINDOW, WINDOW), 1)

    @pl.loop(0, 12)
    def _(i):
        block = i // 4
        head = lax.rem(i, 4)
        row = me * 3 + block
        seg_own = jnp.broadcast_to(SEG[pl.ds(row, 1), :], (WINDOW, WINDOW))
        seg_old = jnp.broadcast_to(SEG[pl.ds(jnp.maximum(row - 1, 0), 1), :], (WINDOW, WINDOW))
        seg_query = jnp.transpose(seg_own)
        old = (seg_query == seg_old) & (k_index > q_index) & (row > 0)
        new = (seg_query == seg_own) & (k_index <= q_index)
        allowed = jnp.concatenate(
            [jnp.where(old, 1.0, 0.0), jnp.where(new, 1.0, 0.0)], axis=1
        ).astype(bf16)
        allowed = jnp.concatenate([allowed, allowed], axis=0)
        q_rows = pl.ds(pl.multiple_of(block * 128, 128), 128)
        k_rows = pl.ds(pl.multiple_of(block * 128, 128), 256)
        k_cols = pl.ds(pl.multiple_of(head * 128, 128), 128)
        kd = KD[k_rows, k_cols]
        vd = jnp.concatenate([VD[k_rows, k_cols], ones], axis=1)
        for p in range(4):
            cols = pl.ds(pl.multiple_of(head * 512 + 128 * p, 128), 128)
            pair = Q[q_rows, cols]
            stacked = jnp.concatenate([pair * keep_a, pair * keep_b], axis=0)
            scores = lax.dot_general(
                stacked, kd, (((1,), (1,)), ((), ())), preferred_element_type=f32
            )
            weights = jnp.exp(softcap * jnp.tanh(scores * (1.0 / softcap))).astype(bf16) * allowed
            mixed = jnp.dot(weights, vd, preferred_element_type=f32)
            mixed = mixed[:, :128] / mixed[:, 128:]
            ATT[q_rows, cols] = jnp.where(first_head, mixed[:128], mixed[128:]).astype(bf16)
        rest(i + 10)

    rest(22)
    go.finish()

    @pl.loop(0, 11)
    def _(i):
        columns = pl.ds(pl.multiple_of(i * 256, 256), 256)
        PRJ[:, columns] = jnp.dot(ATT[...], WO[:, columns], preferred_element_type=f32)

    PRJ[:, pl.ds(2816, 64)] = jnp.dot(ATT[...], WO[:, pl.ds(2816, 64)], preferred_element_type=f32)

    for load in loads[5:]:
        load.wait()

    def verdict_copy(delta, block):
        rows = pl.ds(pl.multiple_of(block * 128, 128), 128)
        ref = VS.at[mem, rows, :]
        return pltpu.make_async_remote_copy(
            src_ref=ref,
            dst_ref=ref,
            send_sem=vs_send,
            recv_sem=vs_recv.at[(delta - 1) * 3 + block],
            device_id={"member": mod(mem + delta, MEM)},
            device_id_type=MESH,
        )

    def res_copy(block):
        rows = pl.ds(pl.multiple_of(block * 128, 128), 128)
        return pltpu.make_async_copy(RES.at[rows, :], res_out.at[rows, :], out_sem.at[block])

    def issue(block):
        res_copy(block).start()
        for delta in (1, 2, 3):
            verdict_copy(delta, block).start()

    @pl.loop(0, 3)
    def _(i):
        for h in range(2):
            rows = pl.ds(pl.multiple_of(i * 128 + 64 * h, 64), 64)
            projected = PRJ[rows, :]
            scale = lax.rsqrt(jnp.mean(projected * projected, axis=-1, keepdims=True) + epsilon)
            updated = (HID[rows, :].astype(f32) + projected * scale * POST[...]).astype(bf16)
            RES[rows, :] = updated
            values = updated.astype(f32)
            scale = lax.rsqrt(jnp.mean(values * values, axis=-1, keepdims=True) + epsilon)
            closing = (values * scale * FIN[...]).astype(bf16)
            verdict = jnp.dot(closing, WJ[...], preferred_element_type=f32)
            VS[mem, rows, :] = verdict.astype(bf16)

        @pl.when(i > 0)
        def _():
            issue(i - 1)

    gq.drain()
    go.drain()
    issue(2)
    for block in range(3):
        for delta in (1, 2, 3):
            verdict_copy(delta, block).wait_recv()
        rows = pl.ds(block * 128, 128)
        total = VS[0, rows, :].astype(f32) + VS[1, rows, :].astype(f32)
        total = total + VS[2, rows, :].astype(f32) + VS[3, rows, :].astype(f32)
        LOG[rows, :] = total * 0.25
    done = pltpu.make_async_copy(LOG, logit_out, out_sem.at[3])
    done.start()
    sent = WO.at[pl.ds(0, 9 * 128), pl.ds(0, 128)]
    pltpu.make_async_copy(sent, sent, vs_send).wait()
    for block in range(3):
        res_copy(block).wait()
    done.wait()


def body(
    hidden, segments, pre_gain, w_query, w_key, w_value, w_output, post_gain, final_gain, w_judge
):
    wqkv = jnp.pad(jnp.concatenate([w_key[0], w_value[0], w_query[0]], axis=1), ((0, 3), (0, 0)))
    dma = pltpu.SemaphoreType.DMA
    any_spec = pl.BlockSpec(memory_space=pl.ANY)
    gather_sems = [dma((3,)), dma((28,)), dma((7,)), dma((24,))]
    updated, logits = pl.pallas_call(
        kernel,
        out_shape=(
            jax.ShapeDtypeStruct((TOK, D), bf16),
            jax.ShapeDtypeStruct((TOK, 128), f32),
        ),
        in_specs=[any_spec] * 8,
        out_specs=(any_spec, any_spec),
        scratch_shapes=[
            pltpu.VMEM((64 * BQ, NQ), bf16),
            pltpu.VMEM((64 * BO, D), bf16),
            pltpu.VMEM((TOK, D), bf16),
            pltpu.VMEM((192, 128), jnp.int32),
            pltpu.VMEM((1, D), f32),
            pltpu.VMEM((1, D), f32),
            pltpu.VMEM((1, D), f32),
            pltpu.VMEM((D, 128), bf16),
            pltpu.VMEM((TOK, 2944), bf16),
            pltpu.VMEM((TOK, 64 * BQ), bf16),
            pltpu.VMEM((TOK, 128), f32),
            pltpu.VMEM((TOK, 128), f32),
            pltpu.VMEM((TOK, QH * HD), bf16),
            pltpu.VMEM((TOK, 512), bf16),
            pltpu.VMEM((WINDOW, 512), bf16),
            pltpu.VMEM((WINDOW + TOK, 512), bf16),
            pltpu.VMEM((WINDOW + TOK, 512), bf16),
            pltpu.VMEM((TOK, QH * HD), bf16),
            pltpu.VMEM((TOK, D), f32),
            pltpu.VMEM((TOK, D), bf16),
            pltpu.VMEM((MEM, TOK, 128), bf16),
            pltpu.VMEM((TOK, 128), f32),
            dma((8,)),
            *gather_sems,
            *gather_sems,
            dma((2,)),
            dma((2,)),
            dma,
            dma,
            dma,
            dma((9,)),
            dma((4,)),
        ],
        compiler_params=pltpu.CompilerParams(
            collective_id=0, has_side_effects=True, vmem_limit_bytes=62 * 1024 * 1024
        ),
    )(
        hidden[0],
        segments.reshape(192, 128),
        pre_gain,
        wqkv,
        w_output[0],
        post_gain,
        final_gain,
        w_judge[0],
    )
    return updated[None], logits


def solution(mesh):
    return jax.shard_map(
        body,
        mesh=mesh,
        in_specs=(
            P("member", "seq", None),
            P(),
            P("member", None),
            P("member", "seq", None),
            P("member", "seq", None),
            P("member", "seq", None),
            P("member", "seq", None),
            P("member", None),
            P("member", None),
            P("member", None, None),
        ),
        out_specs=(P("member", "seq", None), P("seq", None)),
        check_vma=False,
    )
```

time: 460 us -> 124 us (0.27)
  waiting for transfers between devices: 289 us -> 0 us
  Pallas kernels: 0 us -> 112 us
  local copies, waits for them, and re-layouts: 77.1 us -> 9.08 us
  matrix products: 51.4 us -> 0 us
  between operations: 14 us -> 0.65 us
  other arithmetic: 14.2 us -> 1.64 us
  loops' own time: 5.3 us -> 0 us
    all_gather x4 -> x0, waiting for transfers between devices: 246 us -> none  [the longest x1 99.7 us: body(): lax.all_gather(w_query[0], 'seq', axis=0, tiled=True)]
    pallas_call x0 -> x1, Pallas kernels: none -> 112 us  [body(): pl.pallas_call(kernel, out_shape=(jax.ShapeDtypeStruct((TOK, D), bf16), j...]
    dot_general x2 -> x0, local copies, waits for them, and re-layouts: 58.2 us -> none  [the longest x1 50.9 us: body(): jnp.dot(normed, lax.all_gather(w_query[0], 'seq', axis=0, tiled=True), pr...]
    dot_general x13 -> x0, matrix products: 51.4 us -> none  [the longest x4 12.1 us: one_head(): jnp.einsum('qgd,kd->gqk', query_head, key_head, preferred_element_type=jn...]
    psum x1 -> x0, waiting for transfers between devices: 41.7 us -> none  [body(): lax.psum(verdict.astype(jnp.bfloat16), 'member').astype(jnp.float32)]
    dynamic_slice x9 -> x0, local copies, waits for them, and re-layouts: 7.28 us -> none  [the longest x4 4.17 us: one_head(): lax.dynamic_slice_in_dim(block_queries, head_index * head_span, head_span...]
    another operation x1 -> x0, loops' own time: 5.3 us -> none  [attend_heads(): per_head = lax.map(one_head, jnp.arange(KVH, dtype=jnp.int32))]
  transfers between devices with their start and end apart: 7 -> 0, of which waited for: 5 -> 0; matrix products, arithmetic and copies ran while one was open for 27% -> 0% of each run, Pallas kernels for 0% -> 0%
where the time goes in v1:
time: 124 us; the launch traced here: 123 us
  Pallas kernels  112 us (90%)
  local copies, waits for them, and re-layouts  9.08 us (7%)
  other arithmetic  1.64 us (1%)
    pallas_call x1, Pallas kernels, body(): pl.pallas_call(kernel, out_shape=(jax.ShapeDtypeStruct((TOK, D), bf16), j...  112 us
    unnamed x5, local copies, waits for them, and re-layouts  9.08 us

profile of v1, /device:TPU:1, one launch (start us, length us, event | category | flops | bytes accessed | tf_op | source)
XLA Modules:
  0.0 123.4 jit_solution(13261587798698032538)
XLA Ops:
  0.6 1.6 %fusion.4.wqkv = bf16[48,2560]{1,0:T(8,128)(2,1)} fusion(bf16[45,2048]{1,0:T(8,128)(2,1)} %bitcast.11, bf16[45,256]{1,0:T(8,128)(2,1)} %bitcast.14, bf16[45,256]{1,0:T(8,128)(2,1)} %bitcast.15), kind=kLoop, calls=%fused_computation.5 | loop fusion | flops 1228800 | bytes 476160 | tf_op jit(solution)/shard_map/concatenate | solution.py:501
  2.3 4.2 %copy.12 = bf16[1,384,2880]{2,1,0:T(8,128)(2,1)} copy(bf16[1,384,2880]{1,2,0:T(8,128)(2,1)} %param.10) | data formatting | bytes 4423680 | tf_op args[0]
  6.4 112.1 %shard_map.113 = (bf16[384,2880]{1,0:T(8,128)(2,1)}, f32[384,128]{1,0:T(8,128)}) custom-call(bf16[384,2880]{1,0:T(8,128)(2,1)} %bitcast.8, s32[192,128]{1,0:T(8,128)} %bitcast.13, f32[1,2880]{1,0:T(1,128)} %pre_g.1, bf16[48,2560]{1,0:T(8,128)(2,1)} %fusion.4.wqkv, bf16[32,2880]{1,0:T(8,128)(2,1)} %bitcast.12, f32[1,2880]{1,0:T(1,128)} %post_g.1, ...), custom_call_target="tpu_custom_call" | custom-call | tf_op jit(solution)/shard_map/pallas_call | solution.py:505
  118.5 0.0 copy-start
  118.5 4.2 %copy.13 = bf16[1,384,2880]{1,2,0:T(8,128)(2,1)} copy(bf16[1,384,2880]{2,1,0:T(8,128)(2,1)} %bitcast.9) | data formatting | bytes 4423680
  122.8 0.0 copy-done
  122.8 0.7 copy.15
Async XLA Ops:
  118.5 4.2 %copy-start = (f32[384,128]{1,0:T(8,128)S(1)}, f32[384,128]{1,0:T(8,128)}, u32[]{:S(2)}) copy-start(f32[384,128]{1,0:T(8,128)} %get-tuple-element.11) | copy-start | bytes 589828

commit v2 on v1

--- a/solution.py
+++ b/solution.py
@@ -39,15 +39,22 @@
     hid,
     seg,
     pre_g,
-    wqkv,
+    wq,
+    wk,
+    wv,
     wo,
     post_g,
     fin_g,
     wj,
-    res_out,
-    logit_out,
+    RT,
+    LOG,
     WQ,
-    WO,
+    WOX,
+    WOZ,
+    SQ,
+    SK,
+    SV,
+    HT,
     HID,
     SEG,
     PRE,
@@ -64,10 +71,9 @@
     KD,
     VD,
     ATT,
+    ATTZ,
     PRJ,
-    RES,
     VS,
-    LOG,
     local_sem,
     qx,
     qz,
@@ -77,13 +83,14 @@
     oz,
     opz,
     opx,
-    d2d_recv,
+    q_shared,
+    ox_shared,
+    oz_shared,
     send_sem,
     halo_send,
     halo_recv,
     vs_send,
     vs_recv,
-    out_sem,
 ):
     me = lax.axis_index("seq")
     mem = lax.axis_index("member")
@@ -107,18 +114,20 @@
     def local(i, src, dst):
         return pltpu.make_async_copy(src, dst, local_sem.at[i])
 
-    def own(buf, rows):
-        return buf.at[pl.ds(pl.multiple_of(me * rows, rows), rows), :]
-
+    own_x = pl.ds(pl.multiple_of(me * BO, BO), BO)
+    own_z = pl.ds(pl.multiple_of(((x * ZN + z) * 2 + c) * BO, BO), BO)
     loads = [
-        local(0, wqkv, own(WQ, BQ)),
-        local(1, wo, own(WO, BO)),
-        local(2, hid, HID),
-        local(3, pre_g, PRE),
-        local(4, seg, SEG),
-        local(5, post_g, POST),
-        local(6, fin_g, FIN),
-        local(7, wj, WJ),
+        local(0, wk, SK),
+        local(1, wv, SV),
+        local(2, wq, SQ),
+        local(3, hid, HT),
+        local(4, wo.at[:, pl.ds(0, CO)], WOX.at[own_x, :]),
+        local(5, wo.at[:, pl.ds(CO, D - CO)], WOZ.at[own_z, :]),
+        local(6, pre_g, PRE),
+        local(7, seg, SEG),
+        local(8, post_g, POST),
+        local(9, fin_g, FIN),
+        local(10, wj, WJ),
     ]
     for load in loads:
         load.start()
@@ -130,6 +139,11 @@
         pl.semaphore_signal(
             barrier, inc=1, device_id={"member": mod(mem + delta, MEM)}, device_id_type=MESH
         )
+    own_q = pl.ds(pl.multiple_of(me * BQ, BQ), BQ)
+    for load, stage, first, width in ((0, SK, 0, 256), (1, SV, 256, 256), (2, SQ, 512, 2048)):
+        loads[load].wait()
+        padded = jnp.concatenate([stage[...], jnp.zeros((3, width), bf16)], axis=0)
+        WQ[own_q, pl.ds(first, width)] = padded
     pl.semaphore_wait(barrier, 9)
 
     def z_order(i):
@@ -139,22 +153,21 @@
         return mod(x + s * ((i + 1) // 2) * (1 - 2 * lax.rem(i, 2)), XN)
 
     class Gather:
-        def __init__(self, number, buf, rows, cut, rx, rz, pz, px):
-            self.number, self.buf, self.rows, self.cut = number, buf, rows, cut
-            self.width = buf.shape[1]
+        def __init__(self, number, rows, bufs, shared, rx, rz, pz, px):
+            self.number, self.rows, self.bufs, self.shared = number, rows, bufs, shared
             self.rx, self.rz, self.pz, self.px = rx, rz, pz, px
 
         def block(self, part, zz, xx):
-            first = pl.multiple_of(seq_of(zz, xx, c) * self.rows, self.rows)
-            columns = pl.ds(0, self.cut) if part == 0 else pl.ds(self.cut, self.width - self.cut)
-            return self.buf.at[pl.ds(first, self.rows), columns]
+            buf, columns, z_major = self.bufs[part]
+            place = seq_of(zz, xx, c) if z_major else (xx * ZN + zz) * 2 + c
+            return buf.at[pl.ds(pl.multiple_of(place * self.rows, self.rows), self.rows), columns]
 
         def copy(self, part, zz, xx, recv, peer):
             ref = self.block(part, zz, xx)
             return pltpu.make_async_remote_copy(
                 src_ref=ref,
                 dst_ref=ref,
-                send_sem=send_sem.at[self.number],
+                send_sem=send_sem.at[self.number + part],
                 recv_sem=recv,
                 device_id={"seq": peer},
                 device_id_type=MESH,
@@ -167,7 +180,7 @@
             self.copy(part, zz, xx, recv, partner).wait_recv()
 
         def share(self, part, zz, xx):
-            self.send(part, zz, xx, d2d_recv.at[self.number], partner)
+            self.send(part, zz, xx, self.shared[part](zz, xx), partner)
 
         def begin(self):
             self.send(0, z, x, self.rx.at[0], x_f)
@@ -244,22 +257,66 @@
 
                 self.share(0, zb, xj)
 
-        def finish(self):
-            half = self.buf.at[pl.ds(0, 32 * self.rows), :]
-            pltpu.make_async_copy(half, half, d2d_recv.at[self.number]).wait()
-
         def drain(self):
-            sent = self.buf.at[pl.ds(0, 63 * self.rows), :]
-            pltpu.make_async_copy(sent, sent, send_sem.at[self.number]).wait()
-
-    gq = Gather(0, WQ, BQ, CQ, qx, qz, qpz, qpx)
-    go = Gather(1, WO, BO, CO, ox, oz, opz, opx)
-
-    loads[0].wait()
+            for part in range(2):
+                buf, columns, _ = self.bufs[part]
+                sent = buf.at[pl.ds(0, 63 * self.rows), columns]
+                pltpu.make_async_copy(sent, sent, send_sem.at[self.number + part]).wait()
+
+    def arrived(sem, ref):
+        pltpu.make_async_copy(ref, ref, sem).wait()
+
+    gq = Gather(
+        0,
+        BQ,
+        ((WQ, pl.ds(0, CQ), True), (WQ, pl.ds(CQ, NQ - CQ), True)),
+        (lambda zz, xx: q_shared.at[0], lambda zz, xx: q_shared.at[0]),
+        qx,
+        qz,
+        qpz,
+        qpx,
+    )
+    go = Gather(
+        2,
+        BO,
+        ((WOX, slice(None), True), (WOZ, slice(None), False)),
+        (lambda zz, xx: ox_shared.at[zz], lambda zz, xx: oz_shared.at[xx]),
+        ox,
+        oz,
+        opz,
+        opx,
+    )
+
     gq.begin()
 
-    loads[2].wait()
+    lane = lax.broadcasted_iota(jnp.int32, (1, 128), 1)
+    low_half = lax.rem(lane, 64) < 32
+    first_head = lane < 64
+    index = lax.rem(lane, 32).astype(f32)
+    frequency = jnp.exp(index * (-2.0 * math.log(rope_base) / HD))
+    sign = jnp.where(low_half, -1.0, 1.0)
+
+    @pl.loop(0, 3)
+    def _(i):
+        rows = pl.ds(pl.multiple_of(i * 128, 128), 128)
+        position = me * TOK + i * 128 + lax.broadcasted_iota(jnp.int32, (128, 128), 0)
+        angle = position.astype(f32) * frequency
+        COS[rows, :] = jnp.cos(angle)
+        SIN[rows, :] = jnp.sin(angle) * sign
+
     loads[3].wait()
+
+    @pl.loop(0, 7)
+    def _(i):
+        for k in range(3):
+            features = pl.ds(pl.multiple_of(i * 384 + k * 128, 128), 128)
+            HID[:, features] = jnp.transpose(HT[features, :])
+        gq.first(i)
+
+    HID[:, pl.ds(2688, 128)] = jnp.transpose(HT[pl.ds(2688, 128), :])
+    HID[:, pl.ds(2816, 64)] = jnp.transpose(HT[pl.ds(2816, 64), :])
+
+    loads[6].wait()
     NRM[:, pl.ds(2816, 128)] = jnp.zeros((TOK, 128), bf16)
 
     @pl.loop(0, 6)
@@ -268,6 +325,8 @@
         values = HID[rows, :].astype(f32)
         scale = lax.rsqrt(jnp.mean(values * values, axis=-1, keepdims=True) + epsilon)
         NRM[rows, pl.ds(0, D)] = (values * scale * PRE[...]).astype(bf16)
+        PRJ[rows, :] = jnp.zeros((64, D), f32)
+        gq.second(i)
 
     @pl.loop(0, 8)
     def _(t):
@@ -282,47 +341,17 @@
         window = NRM[:, pl.ds(pl.multiple_of(start, 128), 512)]
         moved = jnp.dot(window, pick.astype(bf16), preferred_element_type=f32)
         A[:, pl.ds(pl.multiple_of(t * 384, 384), 384)] = moved.astype(bf16)
-
-        @pl.when(t < 7)
-        def _():
-            gq.first(t)
-
-    lane = lax.broadcasted_iota(jnp.int32, (1, 128), 1)
-    low_half = lax.rem(lane, 64) < 32
-    first_head = lane < 64
-    index = lax.rem(lane, 32).astype(f32)
-    frequency = jnp.exp(index * (-2.0 * math.log(rope_base) / HD))
-    sign = jnp.where(low_half, -1.0, 1.0)
-
-    @pl.loop(0, 3)
-    def _(i):
-        rows = pl.ds(pl.multiple_of(i * 128, 128), 128)
-        position = me * TOK + i * 128 + lax.broadcasted_iota(jnp.int32, (128, 128), 0)
-        angle = position.astype(f32) * frequency
-        COS[rows, :] = jnp.cos(angle)
-        SIN[rows, :] = jnp.sin(angle) * sign
-
-    @pl.loop(0, 10)
+        gq.second(t + 6)
+
+    loads[4].wait()
+    loads[5].wait()
+    go.begin()
+
+    @pl.loop(14, 16)
     def _(r):
         gq.second(r)
 
-    loads[1].wait()
-    go.begin()
-
-    @pl.loop(10, 16)
-    def _(r):
-        gq.second(r)
-
-    gq.finish()
-
-    def rest(slot):
-        @pl.when(slot < 7)
-        def _():
-            go.first(slot)
-
-        @pl.when(slot >= 7)
-        def _():
-            go.second(slot - 7)
+    arrived(q_shared.at[0], WQ.at[pl.ds(0, 32 * BQ), :])
 
     def rotated(half):
         swapped = jnp.where(low_half, pltpu.roll(half, 96, 1), pltpu.roll(half, 32, 1))
@@ -343,14 +372,13 @@
         KV[:, pl.ds(128 * p, 128)] = pair
         for q, both in enumerate(doubled(pair.astype(f32))):
             KD[own_rows, pl.ds(128 * (2 * p + q), 128)] = both.astype(bf16)
-    rest(0)
     vals = project(1)
     for p in range(2):
         pair = vals[:, 128 * p : 128 * p + 128].astype(bf16)
         KV[:, pl.ds(256 + 128 * p, 128)] = pair
         for q, both in enumerate(doubled(pair.astype(f32))):
             VD[own_rows, pl.ds(128 * (2 * p + q), 128)] = both.astype(bf16)
-    rest(1)
+    go.first(0)
 
     halo = pltpu.make_async_remote_copy(
         src_ref=KV.at[pl.ds(TOK - WINDOW, WINDOW), :],
@@ -366,7 +394,10 @@
         for p in range(2):
             half = rotated(tile[:, 128 * p : 128 * p + 128]) * (1.0 / math.sqrt(HD))
             Q[:, pl.ds(pl.multiple_of(i * 256 + 128 * p, 128), 128)] = half.astype(bf16)
-        rest(i + 2)
+
+        @pl.when((i == 2) | (i == 5))
+        def _():
+            go.first((i + 1) // 3)
 
     @pl.loop(0, 1)
     def _(i):
@@ -385,7 +416,7 @@
             for q, both in enumerate(doubled(pair)):
                 store[pl.ds(0, WINDOW), pl.ds(128 * (2 * p + q), 128)] = both.astype(bf16)
 
-    loads[4].wait()
+    loads[7].wait()
     ones = jnp.ones((2 * WINDOW, 128), bf16)
     keep_a = jnp.where(first_head, 1.0, 0.0).astype(bf16)
     keep_b = jnp.where(first_head, 0.0, 1.0).astype(bf16)
@@ -411,6 +442,7 @@
         k_cols = pl.ds(pl.multiple_of(head * 128, 128), 128)
         kd = KD[k_rows, k_cols]
         vd = jnp.concatenate([VD[k_rows, k_cols], ones], axis=1)
+        mixed = []
         for p in range(4):
             cols = pl.ds(pl.multiple_of(head * 512 + 128 * p, 128), 128)
             pair = Q[q_rows, cols]
@@ -419,22 +451,46 @@
                 stacked, kd, (((1,), (1,)), ((), ())), preferred_element_type=f32
             )
             weights = jnp.exp(softcap * jnp.tanh(scores * (1.0 / softcap))).astype(bf16) * allowed
-            mixed = jnp.dot(weights, vd, preferred_element_type=f32)
-            mixed = mixed[:, :128] / mixed[:, 128:]
-            ATT[q_rows, cols] = jnp.where(first_head, mixed[:128], mixed[128:]).astype(bf16)
-        rest(i + 10)
-
-    rest(22)
-    go.finish()
-
-    @pl.loop(0, 11)
-    def _(i):
-        columns = pl.ds(pl.multiple_of(i * 256, 256), 256)
-        PRJ[:, columns] = jnp.dot(ATT[...], WO[:, columns], preferred_element_type=f32)
-
-    PRJ[:, pl.ds(2816, 64)] = jnp.dot(ATT[...], WO[:, pl.ds(2816, 64)], preferred_element_type=f32)
-
-    for load in loads[5:]:
+            both = jnp.dot(weights, vd, preferred_element_type=f32)
+            both = (both[:, :128] / both[:, 128:]).astype(bf16)
+            mixed += [both[:128], both[128:]]
+            ATT[q_rows, cols] = jnp.where(first_head, mixed[2 * p], mixed[2 * p + 1])
+        for k in range(4):
+            cols = pl.ds(pl.multiple_of(k * 512 + head * 128, 128), 128)
+            ATTZ[q_rows, cols] = jnp.where(first_head, mixed[k], mixed[k + 4])
+
+        @pl.when(lax.rem(i, 3) == 2)
+        def _():
+            go.first(i // 3 + 3)
+
+    def add_z_unit(zz):
+        rows = pl.ds(pl.multiple_of(zz * 256, 256), 256)
+        arrived(ox_shared.at[zz], WOX.at[pl.ds(0, 4 * BO), :])
+        PRJ[:, pl.ds(0, CO)] += jnp.dot(ATT[:, rows], WOX[rows, :], preferred_element_type=f32)
+
+    def add_x_unit(xx):
+        rows = pl.ds(pl.multiple_of(xx * 512, 512), 512)
+        arrived(oz_shared.at[xx], WOZ.at[pl.ds(0, 8 * BO), :])
+        PRJ[:, pl.ds(CO, D - CO)] += jnp.dot(
+            ATTZ[:, rows], WOZ[rows, :], preferred_element_type=f32
+        )
+
+    @pl.loop(0, 16)
+    def _(r):
+        go.second(r)
+
+        @pl.when((r == 1) | ((r >= 5) & (r < 9)) | (r == 13) | (r == 14))
+        def _():
+            add_z_unit(z_order(jnp.where(r == 1, 0, jnp.where(r < 9, r - 4, r - 8))))
+
+        @pl.when((r == 0) | (r == 9) | (r == 10))
+        def _():
+            add_x_unit(x_order(jnp.where(r == 0, 0, r - 8)))
+
+    add_z_unit(z_order(7))
+    add_x_unit(x_order(3))
+
+    for load in loads[8:]:
         load.wait()
 
     def verdict_copy(delta, block):
@@ -449,14 +505,11 @@
             device_id_type=MESH,
         )
 
-    def res_copy(block):
-        rows = pl.ds(pl.multiple_of(block * 128, 128), 128)
-        return pltpu.make_async_copy(RES.at[rows, :], res_out.at[rows, :], out_sem.at[block])
-
-    def issue(block):
-        res_copy(block).start()
-        for delta in (1, 2, 3):
-            verdict_copy(delta, block).start()
+    def turn(block, first, count):
+        tokens = pl.ds(pl.multiple_of(block * 128, 128), 128)
+        for k in range(first, first + count):
+            features = pl.ds(128 * k, 128 if k < 22 else 64)
+            RT[features, tokens] = jnp.transpose(NRM[tokens, features])
 
     @pl.loop(0, 3)
     def _(i):
@@ -465,20 +518,19 @@
             projected = PRJ[rows, :]
             scale = lax.rsqrt(jnp.mean(projected * projected, axis=-1, keepdims=True) + epsilon)
             updated = (HID[rows, :].astype(f32) + projected * scale * POST[...]).astype(bf16)
-            RES[rows, :] = updated
+            NRM[rows, pl.ds(0, D)] = updated
             values = updated.astype(f32)
             scale = lax.rsqrt(jnp.mean(values * values, axis=-1, keepdims=True) + epsilon)
             closing = (values * scale * FIN[...]).astype(bf16)
             verdict = jnp.dot(closing, WJ[...], preferred_element_type=f32)
             VS[mem, rows, :] = verdict.astype(bf16)
-
-        @pl.when(i > 0)
-        def _():
-            issue(i - 1)
+        turn(i, 0, 8)
+        for delta in (2, 1, 3):
+            verdict_copy(delta, i).start()
+        turn(i, 8, 15)
 
     gq.drain()
     go.drain()
-    issue(2)
     for block in range(3):
         for delta in (1, 2, 3):
             verdict_copy(delta, block).wait_recv()
@@ -486,78 +538,81 @@
         total = VS[0, rows, :].astype(f32) + VS[1, rows, :].astype(f32)
         total = total + VS[2, rows, :].astype(f32) + VS[3, rows, :].astype(f32)
         LOG[rows, :] = total * 0.25
-    done = pltpu.make_async_copy(LOG, logit_out, out_sem.at[3])
-    done.start()
-    sent = WO.at[pl.ds(0, 9 * 128), pl.ds(0, 128)]
-    pltpu.make_async_copy(sent, sent, vs_send).wait()
-    for block in range(3):
-        res_copy(block).wait()
-    done.wait()
+    sent = WQ.at[pl.ds(0, 9 * 128), pl.ds(0, 128)]
+    arrived(vs_send, sent)
 
 
 def body(
     hidden, segments, pre_gain, w_query, w_key, w_value, w_output, post_gain, final_gain, w_judge
 ):
-    wqkv = jnp.pad(jnp.concatenate([w_key[0], w_value[0], w_query[0]], axis=1), ((0, 3), (0, 0)))
     dma = pltpu.SemaphoreType.DMA
+    vmem = pltpu.VMEM
     any_spec = pl.BlockSpec(memory_space=pl.ANY)
+    vmem_spec = pl.BlockSpec(memory_space=pltpu.VMEM)
     gather_sems = [dma((3,)), dma((28,)), dma((7,)), dma((24,))]
     updated, logits = pl.pallas_call(
         kernel,
         out_shape=(
-            jax.ShapeDtypeStruct((TOK, D), bf16),
-            jax.ShapeDtypeStruct((TOK, 128), f32),
+            vmem((D, TOK), bf16),
+            vmem((TOK, 128), f32),
         ),
-        in_specs=[any_spec] * 8,
-        out_specs=(any_spec, any_spec),
+        in_specs=[any_spec] * 10,
+        out_specs=(vmem_spec, vmem_spec),
         scratch_shapes=[
-            pltpu.VMEM((64 * BQ, NQ), bf16),
-            pltpu.VMEM((64 * BO, D), bf16),
-            pltpu.VMEM((TOK, D), bf16),
-            pltpu.VMEM((192, 128), jnp.int32),
-            pltpu.VMEM((1, D), f32),
-            pltpu.VMEM((1, D), f32),
-            pltpu.VMEM((1, D), f32),
-            pltpu.VMEM((D, 128), bf16),
-            pltpu.VMEM((TOK, 2944), bf16),
-            pltpu.VMEM((TOK, 64 * BQ), bf16),
-            pltpu.VMEM((TOK, 128), f32),
-            pltpu.VMEM((TOK, 128), f32),
-            pltpu.VMEM((TOK, QH * HD), bf16),
-            pltpu.VMEM((TOK, 512), bf16),
-            pltpu.VMEM((WINDOW, 512), bf16),
-            pltpu.VMEM((WINDOW + TOK, 512), bf16),
-            pltpu.VMEM((WINDOW + TOK, 512), bf16),
-            pltpu.VMEM((TOK, QH * HD), bf16),
-            pltpu.VMEM((TOK, D), f32),
-            pltpu.VMEM((TOK, D), bf16),
-            pltpu.VMEM((MEM, TOK, 128), bf16),
-            pltpu.VMEM((TOK, 128), f32),
-            dma((8,)),
+            vmem((64 * BQ, NQ), bf16),
+            vmem((64 * BO, CO), bf16),
+            vmem((64 * BO, D - CO), bf16),
+            vmem((45, 2048), bf16),
+            vmem((45, 256), bf16),
+            vmem((45, 256), bf16),
+            vmem((D, TOK), bf16),
+            vmem((TOK, D), bf16),
+            vmem((192, 128), jnp.int32),
+            vmem((1, D), f32),
+            vmem((1, D), f32),
+            vmem((1, D), f32),
+            vmem((D, 128), bf16),
+            vmem((TOK, 2944), bf16),
+            vmem((TOK, 64 * BQ), bf16),
+            vmem((TOK, 128), f32),
+            vmem((TOK, 128), f32),
+            vmem((TOK, QH * HD), bf16),
+            vmem((TOK, 512), bf16),
+            vmem((WINDOW, 512), bf16),
+            vmem((WINDOW + TOK, 512), bf16),
+            vmem((WINDOW + TOK, 512), bf16),
+            vmem((TOK, QH * HD), bf16),
+            vmem((TOK, QH * HD), bf16),
+            vmem((TOK, D), f32),
+            vmem((MEM, TOK, 128), bf16),
+            dma((11,)),
             *gather_sems,
             *gather_sems,
-            dma((2,)),
-            dma((2,)),
+            dma((1,)),
+            dma((ZN,)),
+            dma((XN,)),
+            dma((4,)),
             dma,
             dma,
             dma,
             dma((9,)),
-            dma((4,)),
         ],
         compiler_params=pltpu.CompilerParams(
-            collective_id=0, has_side_effects=True, vmem_limit_bytes=62 * 1024 * 1024
+            collective_id=0, has_side_effects=True, vmem_limit_bytes=60 * 1024 * 1024
         ),
     )(
-        hidden[0],
+        hidden[0].T,
         segments.reshape(192, 128),
         pre_gain,
-        wqkv,
+        w_query[0],
+        w_key[0],
+        w_value[0],
         w_output[0],
         post_gain,
         final_gain,
         w_judge[0],
     )
-    return updated[None], logits
+    return updated.T[None], logits
 
 
 def solution(mesh):

time: 124 us -> 110 us (0.89)
  local copies, waits for them, and re-layouts: 9.08 us -> 2.04 us
  Pallas kernels: 112 us -> 107 us
  other arithmetic: 1.64 us -> 0 us
    unnamed x5 -> x2, local copies, waits for them, and re-layouts: 9.08 us -> 2.04 us
    pallas_call x1, Pallas kernels: 112 us -> 107 us  [body(): pl.pallas_call(kernel, out_shape=(vmem((D, TOK), bf16), vmem((TOK, 128),...]
    concatenate x1 -> x0, other arithmetic: 1.64 us -> none  [body(): jnp.concatenate([w_key[0], w_value[0], w_query[0]], axis=1)]
where the time goes in v2:
time: 110 us
  Pallas kernels  107 us (97%)
  local copies, waits for them, and re-layouts  2.04 us (2%)
    pallas_call x1, Pallas kernels, body(): pl.pallas_call(kernel, out_shape=(vmem((D, TOK), bf16), vmem((TOK, 128),...  107 us

profile of v2, /device:TPU:1, one launch (start us, length us, event | category | flops | bytes accessed | tf_op | source)
XLA Modules:
  0.0 110.1 jit_solution(14321853027315480936)
XLA Ops:
  0.6 107.4 %shard_map.113 = (bf16[2880,384]{1,0:T(8,128)(2,1)S(1)}, f32[384,128]{1,0:T(8,128)S(1)}) custom-call(bf16[2880,384]{1,0:T(8,128)(2,1)} %bitcast.13, s32[192,128]{1,0:T(8,128)} %bitcast.17, f32[1,2880]{1,0:T(1,128)} %pre_g.1, bf16[45,2048]{1,0:T(8,128)(2,1)} %bitcast.15, bf16[45,256]{1,0:T(8,128)(2,1)} %bitcast.18, bf16[45,256]{1,0:T(8,128)(2,1)} %bitcast.19, ...), custom_call_target="tpu_custom_call" | custom-call | tf_op jit(solution)/shard_map/pallas_call | solution.py:553
  108.0 1.4 %copy.14 = bf16[1,384,2880]{1,2,0:T(8,128)(2,1)} copy(bf16[1,384,2880]{1,2,0:T(8,128)(2,1)S(1)} %bitcast.12) | data formatting | bytes 4423680
  109.4 0.7 copy.15

commit v3 on v2

--- a/solution.py
+++ b/solution.py
@@ -21,6 +21,7 @@
 NQ = KVH * HD * 2 + QH * HD
 CQ = 1024
 CO = 1152
+CL = 2816
 
 epsilon = 1e-06
 softcap = 50.0
@@ -51,9 +52,11 @@
     WQ,
     WOX,
     WOZ,
+    WL,
     SQ,
     SK,
     SV,
+    SL,
     HT,
     HID,
     SEG,
@@ -122,14 +125,15 @@
         local(2, wq, SQ),
         local(3, hid, HT),
         local(4, wo.at[:, pl.ds(0, CO)], WOX.at[own_x, :]),
-        local(5, wo.at[:, pl.ds(CO, D - CO)], WOZ.at[own_z, :]),
+        local(5, wo.at[:, pl.ds(CO, CL - CO)], WOZ.at[own_z, :]),
         local(6, pre_g, PRE),
         local(7, seg, SEG),
         local(8, post_g, POST),
         local(9, fin_g, FIN),
         local(10, wj, WJ),
+        local(11, wo.at[:, pl.ds(CL, D - CL)], SL),
     ]
-    for load in loads:
+    for load in (*loads[:3], loads[11], *loads[3:11]):
         load.start()
 
     barrier = pltpu.get_barrier_semaphore()
@@ -139,10 +143,18 @@
         pl.semaphore_signal(
             barrier, inc=1, device_id={"member": mod(mem + delta, MEM)}, device_id_type=MESH
         )
+    loads[11].wait()
+    last = SL[...].astype(f32)
+    last = jnp.concatenate([last[:16], last[16:]], axis=1)
+    last = jnp.concatenate([last[r : r + 1] for r in range(16)], axis=1).astype(bf16)
     own_q = pl.ds(pl.multiple_of(me * BQ, BQ), BQ)
     for load, stage, first, width in ((0, SK, 0, 256), (1, SV, 256, 256), (2, SQ, 512, 2048)):
         loads[load].wait()
-        padded = jnp.concatenate([stage[...], jnp.zeros((3, width), bf16)], axis=0)
+        if stage is SQ:
+            below = [last, jnp.zeros((2, width), bf16)]
+        else:
+            below = [jnp.zeros((3, width), bf16)]
+        padded = jnp.concatenate([stage[...], *below], axis=0)
         WQ[own_q, pl.ds(first, width)] = padded
     pl.semaphore_wait(barrier, 9)
 
@@ -221,41 +233,68 @@
                 self.share(0, z, xx)
 
         def second(self, r):
-            zz = z_order(lax.rem(r, 8))
-            xx = mod(x - s * (1 + r // 8), XN)
-            self.wait(1, zz, xx, self.px.at[r])
-
-            @pl.when(r < 8)
-            def _():
-                self.send(1, zz, xx, self.px.at[r + 8], x_f)
-
-            self.share(1, zz, xx)
-            xj = x_order(lax.rem(r, 4))
-            zk = mod(z - s * (1 + r // 4), ZN)
-            self.wait(0, zk, xj, self.rz.at[r])
+            odd = lax.rem(r, 2)
 
             @pl.when(r < 12)
             def _():
-                self.send(0, zk, xj, self.rz.at[r + 4], z_f)
-
-            self.share(0, zk, xj)
-
-            @pl.when(r < 8)
-            def _():
-                xb = mod(x + s, XN)
-                self.wait(1, zz, xb, self.px.at[r + 16])
-                self.share(1, zz, xb)
-
-            @pl.when(r < 12)
-            def _():
-                zb = mod(z + s * (1 + r // 4), ZN)
+                xj = x_order(lax.rem(r, 4))
+                k = 1 + r // 4
+                zf = mod(z - s * k, ZN)
+                self.wait(0, zf, xj, self.rz.at[r])
+
+                @pl.when((r < 8) | (odd == 0))
+                def _():
+                    self.send(0, zf, xj, self.rz.at[r + 4], z_f)
+
+                self.share(0, zf, xj)
+                zb = mod(z + s * k, ZN)
                 self.wait(0, zb, xj, self.rz.at[r + 16])
 
                 @pl.when(r < 8)
                 def _():
                     self.send(0, zb, xj, self.rz.at[r + 20], z_b)
 
+                @pl.when((r >= 8) & (odd == 1))
+                def _():
+                    self.send(0, zb, xj, self.rz.at[r + 4], z_b)
+
                 self.share(0, zb, xj)
+
+            @pl.when(r >= 12)
+            def _():
+                for n in range(2):
+                    j = 2 * (r - 12) + n
+                    zz, xj = mod(z + 4, ZN), x_order(j)
+                    self.wait(0, zz, xj, self.rz.at[12 + j])
+                    self.share(0, zz, xj)
+
+            @pl.when(r < 8)
+            def _():
+                zz = z_order(r)
+                xf = mod(x - s, XN)
+                self.wait(1, zz, xf, self.px.at[r])
+
+                @pl.when(odd == 0)
+                def _():
+                    self.send(1, zz, xf, self.px.at[r + 8], x_f)
+
+                self.share(1, zz, xf)
+                xb = mod(x + s, XN)
+                self.wait(1, zz, xb, self.px.at[r + 16])
+
+                @pl.when(odd == 1)
+                def _():
+                    self.send(1, zz, xb, self.px.at[r + 8], x_b)
+
+                self.share(1, zz, xb)
+
+            @pl.when((r >= 8) & (r < 12))
+            def _():
+                for n in range(2):
+                    i = 2 * (r - 8) + n
+                    zz, xx = z_order(i), mod(x + 2, XN)
+                    self.wait(1, zz, xx, self.px.at[8 + i])
+                    self.share(1, zz, xx)
 
         def drain(self):
             for part in range(2):
@@ -341,15 +380,14 @@
         window = NRM[:, pl.ds(pl.multiple_of(start, 128), 512)]
         moved = jnp.dot(window, pick.astype(bf16), preferred_element_type=f32)
         A[:, pl.ds(pl.multiple_of(t * 384, 384), 384)] = moved.astype(bf16)
+
+        @pl.when(t == 6)
+        def _():
+            loads[4].wait()
+            loads[5].wait()
+            go.begin()
+
         gq.second(t + 6)
-
-    loads[4].wait()
-    loads[5].wait()
-    go.begin()
-
-    @pl.loop(14, 16)
-    def _(r):
-        gq.second(r)
 
     arrived(q_shared.at[0], WQ.at[pl.ds(0, 32 * BQ), :])
 
@@ -378,7 +416,6 @@
         KV[:, pl.ds(256 + 128 * p, 128)] = pair
         for q, both in enumerate(doubled(pair.astype(f32))):
             VD[own_rows, pl.ds(128 * (2 * p + q), 128)] = both.astype(bf16)
-    go.first(0)
 
     halo = pltpu.make_async_remote_copy(
         src_ref=KV.at[pl.ds(TOK - WINDOW, WINDOW), :],
@@ -395,26 +432,20 @@
             half = rotated(tile[:, 128 * p : 128 * p + 128]) * (1.0 / math.sqrt(HD))
             Q[:, pl.ds(pl.multiple_of(i * 256 + 128 * p, 128), 128)] = half.astype(bf16)
 
-        @pl.when((i == 2) | (i == 5))
+        @pl.when((i == 3) | (i == 6))
         def _():
-            go.first((i + 1) // 3)
+            go.first(i // 3)
 
     @pl.loop(0, 1)
     def _(i):
         query_tile(i)
 
     halo.start()
+    go.first(0)
 
     @pl.loop(1, 8)
     def _(i):
         query_tile(i)
-
-    halo.wait()
-    for p in range(2):
-        for source, store in ((0, KD), (256, VD)):
-            pair = HALO[:, pl.ds(source + 128 * p, 128)].astype(f32)
-            for q, both in enumerate(doubled(pair)):
-                store[pl.ds(0, WINDOW), pl.ds(128 * (2 * p + q), 128)] = both.astype(bf16)
 
     loads[7].wait()
     ones = jnp.ones((2 * WINDOW, 128), bf16)
@@ -423,9 +454,8 @@
     q_index = lax.broadcasted_iota(jnp.int32, (WINDOW, WINDOW), 0)
     k_index = lax.broadcasted_iota(jnp.int32, (WINDOW, WINDOW), 1)
 
-    @pl.loop(0, 12)
-    def _(i):
-        block = i // 4
+    def attend(i):
+        block = lax.rem(i // 4 + 1, 3)
         head = lax.rem(i, 4)
         row = me * 3 + block
         seg_own = jnp.broadcast_to(SEG[pl.ds(row, 1), :], (WINDOW, WINDOW))
@@ -459,9 +489,27 @@
             cols = pl.ds(pl.multiple_of(k * 512 + head * 128, 128), 128)
             ATTZ[q_rows, cols] = jnp.where(first_head, mixed[k], mixed[k + 4])
 
-        @pl.when(lax.rem(i, 3) == 2)
+    @pl.loop(0, 8)
+    def _(i):
+        attend(i)
+
+        @pl.when((i == 2) | (i == 5))
         def _():
             go.first(i // 3 + 3)
+
+    go.first(5)
+    halo.wait()
+    for p in range(2):
+        for source, store in ((0, KD), (256, VD)):
+            pair = HALO[:, pl.ds(source + 128 * p, 128)].astype(f32)
+            for q, both in enumerate(doubled(pair)):
+                store[pl.ds(0, WINDOW), pl.ds(128 * (2 * p + q), 128)] = both.astype(bf16)
+
+    @pl.loop(8, 12)
+    def _(i):
+        attend(i)
+
+    go.first(6)
 
     def add_z_unit(zz):
         rows = pl.ds(pl.multiple_of(zz * 256, 256), 256)
@@ -471,26 +519,50 @@
     def add_x_unit(xx):
         rows = pl.ds(pl.multiple_of(xx * 512, 512), 512)
         arrived(oz_shared.at[xx], WOZ.at[pl.ds(0, 8 * BO), :])
-        PRJ[:, pl.ds(CO, D - CO)] += jnp.dot(
+        PRJ[:, pl.ds(CO, CL - CO)] += jnp.dot(
             ATTZ[:, rows], WOZ[rows, :], preferred_element_type=f32
         )
 
-    @pl.loop(0, 16)
+    def unpack_last(d):
+        rows = pl.ds(pl.multiple_of(d * BQ + 32, 16), 16)
+        packed = WQ[rows, pl.ds(512, 2048)].astype(f32)[13:14]
+        packed = jnp.concatenate([packed[:, 128 * r : 128 * r + 128] for r in range(16)], axis=0)
+        low = jnp.where(first_head, packed, 0.0)
+        high = jnp.where(first_head, 0.0, packed)
+        WL[pl.ds(pl.multiple_of(d * BO, 16), 16), :] = low.astype(bf16)
+        WL[pl.ds(pl.multiple_of(d * BO + 16, 16), 16), :] = high.astype(bf16)
+
+    def add_last():
+        both = jnp.dot(ATT[...], WL[...], preferred_element_type=f32)
+        PRJ[:, pl.ds(CL, D - CL)] = (both + pltpu.roll(both, 64, 1))[:, : D - CL]
+
+    @pl.loop(0, 14)
     def _(r):
         go.second(r)
 
-        @pl.when((r == 1) | ((r >= 5) & (r < 9)) | (r == 13) | (r == 14))
+        @pl.when((r == 2) | (r == 3))
         def _():
-            add_z_unit(z_order(jnp.where(r == 1, 0, jnp.where(r < 9, r - 4, r - 8))))
-
-        @pl.when((r == 0) | (r == 9) | (r == 10))
+            @pl.loop(0, 8)
+            def _(k):
+                for j in range(4):
+                    unpack_last((r - 2) * 32 + k * 4 + j)
+
+        @pl.when(r == 6)
         def _():
-            add_x_unit(x_order(jnp.where(r == 0, 0, r - 8)))
+            add_last()
+
+        @pl.when((r == 1) | (r == 4) | (r == 5) | (r == 8) | (r == 9) | (r >= 12))
+        def _():
+            add_z_unit(z_order(jnp.where(r == 1, 0, jnp.where(r < 6, r - 3, jnp.where(r < 10, r - 5, r - 7)))))
+
+        @pl.when((r == 0) | (r == 10) | (r == 11))
+        def _():
+            add_x_unit(x_order(jnp.where(r == 0, 0, r - 9)))
 
     add_z_unit(z_order(7))
     add_x_unit(x_order(3))
 
-    for load in loads[8:]:
+    for load in loads[8:11]:
         load.wait()
 
     def verdict_copy(delta, block):
@@ -561,10 +633,12 @@
         scratch_shapes=[
             vmem((64 * BQ, NQ), bf16),
             vmem((64 * BO, CO), bf16),
-            vmem((64 * BO, D - CO), bf16),
+            vmem((64 * BO, CL - CO), bf16),
+            vmem((64 * BO, 128), bf16),
             vmem((45, 2048), bf16),
             vmem((45, 256), bf16),
             vmem((45, 256), bf16),
+            vmem((BO, D - CL), bf16),
             vmem((D, TOK), bf16),
             vmem((TOK, D), bf16),
             vmem((192, 128), jnp.int32),
@@ -585,7 +659,7 @@
             vmem((TOK, QH * HD), bf16),
             vmem((TOK, D), f32),
             vmem((MEM, TOK, 128), bf16),
-            dma((11,)),
+            dma((12,)),
             *gather_sems,
             *gather_sems,
             dma((1,)),

time: 110 us -> 109 us (level)
  no operation moved by 1% of the time
where the time goes in v3:
time: 109 us
  Pallas kernels  107 us (98%)
  local copies, waits for them, and re-layouts  2.04 us (2%)
    pallas_call x1, Pallas kernels, body(): pl.pallas_call(kernel, out_shape=(vmem((D, TOK), bf16), vmem((TOK, 128),...  107 us

profile of v3, /device:TPU:1, one launch (start us, length us, event | category | flops | bytes accessed | tf_op | source)
XLA Modules:
  0.0 109.2 jit_solution(10784997554436085094)
XLA Ops:
  0.6 106.5 %shard_map.113 = (bf16[2880,384]{1,0:T(8,128)(2,1)S(1)}, f32[384,128]{1,0:T(8,128)S(1)}) custom-call(bf16[2880,384]{1,0:T(8,128)(2,1)} %bitcast.13, s32[192,128]{1,0:T(8,128)} %bitcast.17, f32[1,2880]{1,0:T(1,128)} %pre_g.1, bf16[45,2048]{1,0:T(8,128)(2,1)} %bitcast.15, bf16[45,256]{1,0:T(8,128)(2,1)} %bitcast.18, bf16[45,256]{1,0:T(8,128)(2,1)} %bitcast.19, ...), custom_call_target="tpu_custom_call" | custom-call | tf_op jit(solution)/shard_map/pallas_call | solution.py:625
  107.1 1.4 %copy.14 = bf16[1,384,2880]{1,2,0:T(8,128)(2,1)} copy(bf16[1,384,2880]{1,2,0:T(8,128)(2,1)S(1)} %bitcast.12) | data formatting | bytes 4423680
  108.5 0.7 copy.15

commit v4 on v3

--- a/solution.py
+++ b/solution.py
@@ -20,7 +20,7 @@
 BO = 32
 NQ = KVH * HD * 2 + QH * HD
 CQ = 1024
-CO = 1152
+CO = 896
 CL = 2816
 
 epsilon = 1e-06
@@ -133,7 +133,7 @@
         local(10, wj, WJ),
         local(11, wo.at[:, pl.ds(CL, D - CL)], SL),
     ]
-    for load in (*loads[:3], loads[11], *loads[3:11]):
+    for load in (*loads[:3], loads[11]):
         load.start()
 
     barrier = pltpu.get_barrier_semaphore()
@@ -143,6 +143,9 @@
         pl.semaphore_signal(
             barrier, inc=1, device_id={"member": mod(mem + delta, MEM)}, device_id_type=MESH
         )
+    for load in loads[3:11]:
+        load.start()
+
     loads[11].wait()
     last = SL[...].astype(f32)
     last = jnp.concatenate([last[:16], last[16:]], axis=1)
@@ -551,16 +554,16 @@
         def _():
             add_last()
 
-        @pl.when((r == 1) | (r == 4) | (r == 5) | (r == 8) | (r == 9) | (r >= 12))
+        @pl.when((r == 1) | (r == 4) | (r == 5) | (r >= 10))
         def _():
-            add_z_unit(z_order(jnp.where(r == 1, 0, jnp.where(r < 6, r - 3, jnp.where(r < 10, r - 5, r - 7)))))
-
-        @pl.when((r == 0) | (r == 10) | (r == 11))
+            add_z_unit(z_order(jnp.where(r == 1, 0, jnp.where(r < 6, r - 3, r - 7))))
+
+        @pl.when((r == 0) | (r == 8) | (r == 9))
         def _():
-            add_x_unit(x_order(jnp.where(r == 0, 0, r - 9)))
-
+            add_x_unit(x_order(jnp.where(r == 0, 0, r - 7)))
+
+    add_x_unit(x_order(3))
     add_z_unit(z_order(7))
-    add_x_unit(x_order(3))
 
     for load in loads[8:11]:
         load.wait()
@@ -577,6 +580,10 @@
             device_id_type=MESH,
         )
 
+    def issue(block):
+        for delta in (2, 1, 3):
+            verdict_copy(delta, block).start()
+
     def turn(block, first, count):
         tokens = pl.ds(pl.multiple_of(block * 128, 128), 128)
         for k in range(first, first + count):
@@ -596,10 +603,18 @@
             closing = (values * scale * FIN[...]).astype(bf16)
             verdict = jnp.dot(closing, WJ[...], preferred_element_type=f32)
             VS[mem, rows, :] = verdict.astype(bf16)
-        turn(i, 0, 8)
-        for delta in (2, 1, 3):
-            verdict_copy(delta, i).start()
-        turn(i, 8, 15)
+
+        @pl.when(i > 0)
+        def _():
+            issue(i - 1)
+
+    turn(0, 0, 4)
+    issue(2)
+    turn(0, 4, 19)
+
+    @pl.loop(1, 3)
+    def _(i):
+        turn(i, 0, 23)
 
     gq.drain()
     go.drain()

time: 109 us -> 108 us (level)
  Pallas kernels: 107 us -> 105 us
    pallas_call x1, Pallas kernels: 107 us -> 105 us  [body(): pl.pallas_call(kernel, out_shape=(vmem((D, TOK), bf16), vmem((TOK, 128),...]
where the time goes in v4:
time: 108 us
  Pallas kernels  105 us (97%)
  local copies, waits for them, and re-layouts  2.04 us (2%)
    pallas_call x1, Pallas kernels, body(): pl.pallas_call(kernel, out_shape=(vmem((D, TOK), bf16), vmem((TOK, 128),...  105 us

profile of v4, /device:TPU:1, one launch (start us, length us, event | category | flops | bytes accessed | tf_op | source)
XLA Modules:
  0.0 107.9 jit_solution(10637253011940296328)
XLA Ops:
  0.6 105.2 %shard_map.113 = (bf16[2880,384]{1,0:T(8,128)(2,1)S(1)}, f32[384,128]{1,0:T(8,128)S(1)}) custom-call(bf16[2880,384]{1,0:T(8,128)(2,1)} %bitcast.13, s32[192,128]{1,0:T(8,128)} %bitcast.17, f32[1,2880]{1,0:T(1,128)} %pre_g.1, bf16[45,2048]{1,0:T(8,128)(2,1)} %bitcast.15, bf16[45,256]{1,0:T(8,128)(2,1)} %bitcast.18, bf16[45,256]{1,0:T(8,128)(2,1)} %bitcast.19, ...), custom_call_target="tpu_custom_call" | custom-call | tf_op jit(solution)/shard_map/pallas_call | solution.py:640
  105.9 1.4 %copy.14 = bf16[1,384,2880]{1,2,0:T(8,128)(2,1)} copy(bf16[1,384,2880]{1,2,0:T(8,128)(2,1)S(1)} %bitcast.12) | data formatting | bytes 4423680
  107.2 0.7 copy.15
